TPU v7x, 256 devices: a whole 4x4x8 slice. The times are simulated.
256 devices in a mesh: dp: 16 (over x_hi, y, core), seq: 16 (over z, x_lo).
Axes of the slice: x: 4 (x_hi: 2, x_lo: 2; x = x_hi * 2 + x_lo), y: 4, z: 8, core: 2. Of those that a mesh axis runs over, the one named last changes fastest.
Arguments:
- layer_input: bfloat16 [16, 2048, 5120], P('dp', 'seq'), may hold values from -6 to 6
- query_states: bfloat16 [16, 2048, 2560], P('dp', 'seq'), may hold values from -24 to 24
- key_states: bfloat16 [16, 2048, 512], P('dp', 'seq'), may hold values from -6 to 6
- out_grad: bfloat16 [16, 2048, 2560], P('dp', 'seq'), may hold values from -12 to 12
- value_weight: bfloat16 [5120, 512], P('dp'), may hold values from -0.078125 to 0.078125
- segment_ids: int32 [16, 2048], P('dp'), may hold values from 0 to 31, as said below
- pair_split: int32 [16, 32], P('dp'), may hold values from 1 to 2047, as said below
Outputs:
- query_grad: bfloat16 [16, 2048, 2560], P('dp', 'seq')
- key_grad: bfloat16 [16, 2048, 512], P('dp', 'seq')
- input_grad: bfloat16 [16, 2048, 5120], P('dp', 'seq')
- weight_grad: float32 [5120, 512], P('dp', 'seq')
Inputs may be any that keep to these rules, and one draw needn't show every extreme that they name: `segment_ids`: each packed row holds 32 sentence pairs numbered 0 to 31 in order along the row; each pair has 16 to 112 positions, every row has a pair of exactly 112, and the pair lengths of a row can be matched two by two into sums of 128. pair_split[r, s] lies after the first position of pair s and at or before its last position; in every row the first pair's second sentence begins at position 1 and the last pair's at position 2047.
All inputs are finite; a program needn't handle non-finite values.
Results may differ from a plain program's by a relative error of at most 0.0057.
Values may be sent and summed in bfloat16 or wider, within the bound.
A program may use at most 128 MiB of HBM per device.

v0:
```python
import jax
import jax.numpy as jnp
from jax import lax
from jax.sharding import PartitionSpec as P

HD = 128


def with_halo(cells, sides, width):
    for axis, dim in sides:
        count = lax.axis_size(axis)
        ends = count - 1
        head = lax.slice_in_dim(cells, 0, width, axis=dim)
        tail = lax.slice_in_dim(cells, cells.shape[dim] - width, cells.shape[dim], axis=dim)
        cells = jnp.concatenate(
            [
                lax.ppermute(tail, axis, [(i, (i + 1) % count) for i in range(ends)]),
                cells,
                lax.ppermute(head, axis, [((i + 1) % count, i) for i in range(ends)]),
            ],
            axis=dim,
        )
    return cells


def passed_along(array, axis, by):
    count = lax.axis_size(axis)
    pairs = [(i, i + by) for i in range(count) if 0 <= i + by < count]
    return lax.ppermute(array, axis, pairs)


def attend_block(query_rows, key_rows, value_rows, grad_rows, visible):
    rows_here = query_rows.shape[0]
    keys_here = key_rows.shape[0]
    head_count = key_rows.shape[1] // HD
    group_size = query_rows.shape[1] // key_rows.shape[1]
    score_scale = HD ** (-0.5)
    high = lax.Precision.HIGHEST
    query_split = query_rows.reshape(rows_here, head_count, group_size, HD)
    grad_split = grad_rows.reshape(rows_here, head_count, group_size, HD)
    key_split = key_rows.reshape(keys_here, head_count, HD)
    value_split = value_rows.reshape(keys_here, head_count, HD)
    query_parts = []
    key_parts = []
    value_parts = []
    for kv_group in range(head_count):
        query_head = query_split[:, kv_group]
        grad_head = grad_split[:, kv_group]
        key_head = key_split[:, kv_group]
        value_head = value_split[:, kv_group]
        scores = (
            jnp.einsum("qgd,kd->gqk", query_head, key_head, preferred_element_type=jnp.float32)
            * score_scale
        )
        masked = jnp.where(visible[None], scores, -1e30)
        highest = jnp.max(masked, axis=-1, keepdims=True)
        weights = jnp.where(visible[None], jnp.exp(masked - highest), 0.0)
        attention = weights / jnp.sum(weights, axis=-1, keepdims=True)
        attention_low = attention.astype(jnp.bfloat16)
        prob_grad = jnp.einsum(
            "qgd,kd->gqk", grad_head, value_head, preferred_element_type=jnp.float32
        )
        row_delta = jnp.sum(attention * prob_grad, axis=-1, keepdims=True)
        score_grad = attention * (prob_grad - row_delta)
        key_wide = key_head.astype(jnp.float32)
        query_wide = query_head.astype(jnp.float32)
        query_parts.append(
            jnp.einsum("gqk,kd->qgd", score_grad, key_wide, precision=high) * score_scale
        )
        key_parts.append(
            jnp.einsum("gqk,qgd->kd", score_grad, query_wide, precision=high) * score_scale
        )
        value_parts.append(
            jnp.einsum("gqk,qgd->kd", attention_low, grad_head, preferred_element_type=jnp.float32)
        )
    query_grad = jnp.stack(query_parts, axis=1).reshape(rows_here, -1)
    kv_grad = jnp.concatenate(key_parts + value_parts, axis=1)
    return (query_grad, kv_grad)


def local(layer_input, query_states, key_states, out_grad, value_weight, segment_ids, pair_split):
    layer_rows = layer_input[0]
    tok_count = layer_rows.shape[0]
    kv_width = key_states.shape[2]
    row_base = lax.axis_index("seq") * tok_count
    columns = layer_rows
    value_rows = jnp.dot(
        columns,
        lax.all_gather(value_weight, "dp", axis=0, tiled=True),
        preferred_element_type=jnp.float32,
    )
    value_low = value_rows.astype(jnp.bfloat16)
    both_states = jnp.concatenate([key_states[0], value_low], axis=1)
    extended = with_halo(both_states, (("seq", 0),), tok_count)
    key_block = extended[:, :kv_width]
    value_block = extended[:, kv_width:]
    seg_row = segment_ids[0]
    fill_ids = jnp.full((tok_count,), -1, jnp.int32)
    padded_ids = jnp.concatenate([fill_ids, seg_row, fill_ids])
    seg_key = lax.dynamic_slice_in_dim(padded_ids, row_base, tok_count + 2 * tok_count, 0)
    seg_query = lax.dynamic_slice_in_dim(seg_row, row_base, tok_count, 0)
    pair_numbers = jnp.arange(pair_split.shape[1], dtype=jnp.int32)
    split_query = jnp.sum(
        jnp.where(seg_query[:, None] == pair_numbers[None, :], pair_split[0][None, :], 0), axis=1
    )
    pos_query = row_base + jnp.arange(tok_count, dtype=jnp.int32)
    pos_key = row_base - tok_count + jnp.arange(tok_count + 2 * tok_count, dtype=jnp.int32)
    visible = (seg_key[None, :] == seg_query[:, None]) & (
        (pos_key[None, :] <= pos_query[:, None]) | (pos_key[None, :] < split_query[:, None])
    )
    query_grad, kv_grad = attend_block(
        query_states[0], key_block, value_block, out_grad[0], visible
    )
    lower_rim = kv_grad[:tok_count]
    upper_rim = kv_grad[tok_count + tok_count :]
    center = kv_grad[tok_count : tok_count + tok_count]
    from_upper = passed_along(lower_rim, "seq", -1)
    from_lower = passed_along(upper_rim, "seq", 1)
    center = center + from_upper + from_lower
    key_grad = center[:, :kv_width].astype(jnp.bfloat16)
    value_grad = center[:, kv_width:].astype(jnp.bfloat16)
    input_grad = lax.dot_general(
        value_grad,
        lax.all_gather(value_weight, "dp", axis=0, tiled=True),
        (((1,), (1,)), ((), ())),
        preferred_element_type=jnp.float32,
    )
    columns = layer_rows
    own_rows = lax.psum_scatter(
        lax.dot_general(
            columns, value_grad, (((0,), (0,)), ((), ())), preferred_element_type=jnp.float32
        ),
        "dp",
        scatter_dimension=0,
        tiled=True,
    )
    summed = lax.psum_scatter(own_rows, "seq", scatter_dimension=1, tiled=True)
    devices_all = lax.axis_size("dp") * lax.axis_size("seq")
    weight_grad = summed / devices_all
    return (
        query_grad.astype(jnp.bfloat16)[None],
        key_grad[None],
        input_grad.astype(jnp.bfloat16)[None],
        weight_grad,
    )


def solution(mesh):
    return jax.shard_map(
        local,
        mesh=mesh,
        in_specs=(
            P("dp", "seq", None),
            P("dp", "seq", None),
            P("dp", "seq", None),
            P("dp", "seq", None),
            P("dp", None),
            P("dp", None),
            P("dp", None),
        ),
        out_specs=(
            P("dp", "seq", None),
            P("dp", "seq", None),
            P("dp", "seq", None),
            P("dp", "seq"),
        ),
        check_vma=False,
    )
```

profile of v0, /device:TPU:16, one launch (start us, length us, event | category | flops | bytes accessed | tf_op | source)
XLA Modules:
  0.0 368.2 jit_solution(11370934144328889524)
XLA Ops:
  10.2 66.7 %all-gather.2.cloned.1.call-done = bf16[5120,512]{1,0:T(8,128)(2,1)} async-done(((bf16[320,512]{1,0:T(8,128)(2,1)}), bf16[5120,512]{1,0:T(8,128)(2,1)}) %all-gather.2.cloned.1.call-update) | async-done | bytes 5242896 | tf_op jit(solution)/shard_map/all_gather | solution.py:89
  76.8 3.3 fusion.36
  80.9 1.3 collective-permute-start.1
  82.2 5.3 %collective-permute-start = (bf16[128,1024]{1,0:T(8,128)(2,1)}, bf16[128,1024]{1,0:T(8,128)(2,1)}, u32[]{:S(2)}, u32[]{:S(2)}) collective-permute-start(bf16[128,1024]{1,0:T(8,128)(2,1)} %pad_maximum_fusion.2), channel_id=1, source_target_pairs={{0,1},{1,2},{2,3},{3,4},{4,5},{5,6},{6,7},{7,8},{8,9},{9,10},{10,1... | collective-permute-start | bytes 786440 | tf_op jit(solution)/shard_map/ppermute | solution.py:17
  88.3 1.1 copy.137
  90.2 1.4 collective-permute-done.1
  91.6 4.6 %collective-permute-done = bf16[128,1024]{1,0:T(8,128)(2,1)} collective-permute-done((bf16[128,1024]{1,0:T(8,128)(2,1)}, bf16[128,1024]{1,0:T(8,128)(2,1)}, u32[]{:S(2)}, u32[]{:S(2)}) %collective-permute-start) | collective-permute-done | bytes 262176 | tf_op jit(solution)/shard_map/ppermute | solution.py:17
  96.2 1.1 pad_maximum_fusion
  97.6 1.4 fusion.76
  99.5 1.4 fusion.80
  101.0 1.4 fusion.79
  102.4 1.4 fusion.78
  103.8 1.4 fusion.77
  105.3 1.6 multiply_reduce_fusion.3
  114.7 1.8 fusion.35
  116.5 1.8 fusion.34
  118.3 1.8 fusion.33
  120.1 1.8 fusion.32
  122.0 1.3 collective-permute-start.2
  123.3 5.2 %collective-permute-start.3 = (f32[128,1024]{0,1:T(8,128)S(1)}, f32[128,1024]{0,1:T(8,128)S(1)}, u32[]{:S(2)}, u32[]{:S(2)}) collective-permute-start(f32[128,1024]{0,1:T(8,128)S(1)} %get-tuple-element.21), channel_id=1, source_target_pairs={{0,1},{1,2},{2,3},{3,4},{4,5},{5,6},{6,7},{7,8},{8,9},{9,10},{10,1... | collective-permute-start | bytes 1572872 | tf_op jit(solution)/shard_map/ppermute | solution.py:29
  128.5 9.9 %collective-permute-done.2 = f32[128,1024]{0,1:T(8,128)S(1)} collective-permute-done((f32[128,1024]{0,1:T(8,128)S(1)}, f32[128,1024]{0,1:T(8,128)S(1)}, u32[]{:S(2)}, u32[]{:S(2)}) %collective-permute-start.2) | collective-permute-done | bytes 524320 | tf_op jit(solution)/shard_map/ppermute | solution.py:29
  138.5 11.4 %collective-permute-done.3 = f32[128,1024]{0,1:T(8,128)S(1)} collective-permute-done((f32[128,1024]{0,1:T(8,128)S(1)}, f32[128,1024]{0,1:T(8,128)S(1)}, u32[]{:S(2)}, u32[]{:S(2)}) %collective-permute-start.3) | collective-permute-done | bytes 524320 | tf_op jit(solution)/shard_map/ppermute | solution.py:29
  149.9 5.3 %convolution_bitcast_fusion = f32[5120,512]{0,1:T(8,128)} fusion(bf16[1,128,5120]{2,1,0:T(8,128)(2,1)S(1)} %copy-done, bf16[128,1024]{0,1:T(8,128)(2,1)S(1)} %fusion.52), kind=kOutput, calls=%fused_computation.4 | convolution fusion | flops 671088640 | bytes 11927552 | tf_op jit(solution)/shard_map/dot_general | solution.py:130
  155.3 11.4 %copy.205 = f32[5120,512]{1,0:T(8,128)} copy(f32[5120,512]{0,1:T(8,128)} %convolution_bitcast_fusion) | data formatting | bytes 20971520
  167.6 2.2 fusion.50
  169.8 116.5 %reduce-scatter.7.cloned.1.call-done = f32[320,512]{1,0:T(8,128)} async-done(((f32[5120,512]{1,0:T(8,128)}), f32[320,512]{1,0:T(8,128)}) %reduce-scatter.7.cloned.1.call-update) | async-done | bytes 655376
  286.2 2.2 copy.206
  288.6 2.3 fusion.49
  293.3 1.1 copy.175
  295.2 5.4 %fusion.4 = bf16[1,128,5120]{2,1,0:T(8,128)(2,1)} fusion(bf16[5120,512]{1,0:T(8,128)(2,1)} %all-gather.2.cloned.1.call-done, bf16[128,1024]{0,1:T(8,128)(2,1)S(1)} %fusion.52), kind=kOutput, calls=%fused_computation.6 | convolution fusion | flops 671744000 | bytes 6684672 | tf_op jit(solution)/shard_map/dot_general | solution.py:122
  300.6 59.7 %reduce-scatter.5.cloned.1.call-done = f32[320,32]{0,1:T(8,128)} async-done(((f32[320,512]{0,1:T(8,128)}), f32[320,32]{0,1:T(8,128)}) %reduce-scatter.5.cloned.1.call-update) | async-done | bytes 40976 | tf_op jit(solution)/shard_map/reduce_scatter | solution.py:137
  360.3 1.4 broadcast_multiply_fusion
  (106 shorter events, 18.0 us)
Async XLA Ops:
  7.2 69.7 %copy-start = (bf16[1,128,5120]{2,1,0:T(8,128)(2,1)S(1)}, bf16[1,128,5120]{2,1,0:T(8,128)(2,1)}, u32[]{:S(2)}) copy-start(bf16[1,128,5120]{2,1,0:T(8,128)(2,1)} %param.7) | copy-start | bytes 3932164
  7.2 69.6 %all-gather.2.cloned.1.call-start = ((), (), s32[]{:S(2)}) async-start(), calls=%async_computation.2 | async-start | bytes 5570560 | tf_op jit(solution)/shard_map/all_gather | solution.py:89
  7.9 278.3 %reduce-scatter.7.cloned.1.call-start = ((), (), s32[]{:S(2)}) async-start(), calls=%async_computation.4 | async-start | bytes 11141120
  10.2 70.0 %copy-start.4 = (bf16[1,128,512]{2,1,0:T(8,128)(2,1)S(1)}, bf16[1,128,512]{2,1,0:T(8,128)(2,1)}, u32[]{:S(2)}) copy-start(bf16[1,128,512]{2,1,0:T(8,128)(2,1)} %param.9) | copy-start | bytes 393220
  10.2 77.8 %copy-start.1 = (bf16[1,128,2560]{2,1,0:T(8,128)(2,1)S(1)}, bf16[1,128,2560]{2,1,0:T(8,128)(2,1)}, u32[]{:S(2)}) copy-start(bf16[1,128,2560]{2,1,0:T(8,128)(2,1)} %param.8) | copy-start | bytes 1966084
  80.2 8.1 %copy-start.2 = (bf16[1,128,2560]{2,1,0:T(8,128)(2,1)S(1)}, bf16[1,128,2560]{2,1,0:T(8,128)(2,1)}, u32[]{:S(2)}) copy-start(bf16[1,128,2560]{2,1,0:T(8,128)(2,1)} %param.10) | copy-start | bytes 1966084
  80.9 10.7 %collective-permute-start.1 = (bf16[128,1024]{1,0:T(8,128)(2,1)}, bf16[128,1024]{1,0:T(8,128)(2,1)}, u32[]{:S(2)}, u32[]{:S(2)}) collective-permute-start(bf16[128,1024]{1,0:T(8,128)(2,1)} %pad_maximum_fusion.2), channel_id=1, source_target_pairs={{1,0},{2,1},{3,2},{4,3},{5,4},{6,5},{7,6},{8,7},{9,8},{10,9},{11,1... | collective-permute-start | bytes 786440 | tf_op jit(solution)/shard_map/ppermute | solution.py:19
  82.2 14.0 %collective-permute-start = (bf16[128,1024]{1,0:T(8,128)(2,1)}, bf16[128,1024]{1,0:T(8,128)(2,1)}, u32[]{:S(2)}, u32[]{:S(2)}) collective-permute-start(bf16[128,1024]{1,0:T(8,128)(2,1)} %pad_maximum_fusion.2), channel_id=1, source_target_pairs={{0,1},{1,2},{2,3},{3,4},{4,5},{5,6},{6,7},{7,8},{8,9},{9,10},{10,1... | collective-permute-start | bytes 786440 | tf_op jit(solution)/shard_map/ppermute | solution.py:17
  90.2 13.6 %copy-start.16 = (pred[128,384]{0,1:T(8,128)(4,1)}, pred[128,384]{0,1:T(8,128)(4,1)S(1)}, u32[]{:S(2)}) copy-start(pred[128,384]{0,1:T(8,128)(4,1)S(1)} %or_and_fusion) | copy-start | bytes 147460
  99.5 2.9 copy-start.9
  99.5 2.9 copy-start.11
  99.5 2.9 copy-start.7
  99.5 4.3 %copy-start.5 = (bf16[384,1,128]{2,1,0:T(2,128)(2,1)}, bf16[384,1,128]{2,1,0:T(2,128)(2,1)S(1)}, u32[]{:S(2)}) copy-start(bf16[384,1,128]{2,1,0:T(2,128)(2,1)S(1)} %get-tuple-element.27) | copy-start | bytes 294916
  105.3 1.7 copy-start.22
  106.9 1.4 copy-start.3
  107.0 1.5 copy-start.15
  107.0 1.8 copy-start.21
  109.1 1.2 copy-start.14
  109.1 1.6 copy-start.19
  111.0 1.6 copy-start.17
  122.0 16.5 %collective-permute-start.2 = (f32[128,1024]{0,1:T(8,128)S(1)}, f32[128,1024]{0,1:T(8,128)S(1)}, u32[]{:S(2)}, u32[]{:S(2)}) collective-permute-start(f32[128,1024]{0,1:T(8,128)S(1)} %get-tuple-element.20), channel_id=1, source_target_pairs={{1,0},{2,1},{3,2},{4,3},{5,4},{6,5},{7,6},{8,7},{9,8},{10,9},{11,1... | collective-permute-start | bytes 1572872 | tf_op jit(solution)/shard_map/ppermute | solution.py:29
  123.3 26.6 %collective-permute-start.3 = (f32[128,1024]{0,1:T(8,128)S(1)}, f32[128,1024]{0,1:T(8,128)S(1)}, u32[]{:S(2)}, u32[]{:S(2)}) collective-permute-start(f32[128,1024]{0,1:T(8,128)S(1)} %get-tuple-element.21), channel_id=1, source_target_pairs={{0,1},{1,2},{2,3},{3,4},{4,5},{5,6},{6,7},{7,8},{8,9},{9,10},{10,1... | collective-permute-start | bytes 1572872 | tf_op jit(solution)/shard_map/ppermute | solution.py:29
  166.7 193.6 %reduce-scatter.5.cloned.1.call-start = ((), (), s32[]{:S(2)}) async-start(), calls=%async_computation.3 | async-start | bytes 835584 | tf_op jit(solution)/shard_map/reduce_scatter | solution.py:137
  169.7 118.8 %copy-start.10 = (bf16[384,1,128]{2,1,0:T(2,128)(2,1)S(1)}, bf16[384,1,128]{2,1,0:T(2,128)(2,1)}, u32[]{:S(2)}) copy-start(bf16[384,1,128]{2,1,0:T(2,128)(2,1)} %copy-done.9) | copy-start | bytes 294916
  169.8 118.8 %copy-start.30 = (f32[5,128]{1,0:T(8,128)S(1)}, f32[5,128]{1,0:T(8,128)}, u32[]{:S(2)}) copy-start(f32[5,128]{1,0:T(8,128)} %copy-done.29) | copy-start | bytes 7684
  288.5 2.4 copy-start.8
  288.5 2.4 copy-start.20
  288.6 2.4 copy-start.25
  288.6 2.4 copy-start.32
  291.0 1.3 copy-start.18
  291.0 1.6 copy-start.27
  291.0 1.6 copy-start.34
  (12 other events, 11.7 us)
Sparse Core Ops, SparseCore 0:
  10.8 65.9 all-gather.1
  166.8 119.4 reduce-scatter.6
  288.8 71.4 reduce-scatter.4
where the time goes:
time: 369 us; the launch traced here: 368 us
  waiting for transfers between devices  271 us (73%)
  matrix products  38.3 us (10%)
  local copies, waits for them, and re-layouts  25.4 us (7%)
  between operations  14.3 us (4%)
  starting transfers between devices  13.2 us (4%)
  other arithmetic  6.26 us (2%)
    unnamed x4, waiting for transfers between devices  117 us
    all_gather x1, waiting for transfers between devices, local(): lax.all_gather(value_weight, 'dp', axis=0, tiled=True)  66.7 us
    reduce_scatter x1, waiting for transfers between devices, local(): summed = lax.psum_scatter(own_rows, 'seq', scatter_dimension=1, tiled=True)  59.7 us
    unnamed x80, local copies, waits for them, and re-layouts  22.4 us
    ppermute x2, waiting for transfers between devices, passed_along(): return lax.ppermute(array, axis, pairs)  21.3 us
  transfers between devices with their start and end apart: 7, of which 7 were waited for; matrix products, arithmetic and copies ran while one was open for 5% of the time, Pallas kernels for 0%

commit v1 on v0

--- a/solution.py
+++ b/solution.py
@@ -2,8 +2,18 @@
 import jax.numpy as jnp
 from jax import lax
 from jax.sharding import PartitionSpec as P
+from jax.lax import all_to_all, axis_size
 
 HD = 128
+
+
+def _part_masks(point, mesh_ax):
+    store = []
+    for _ in range(axis_size(mesh_ax)):
+        store.append(point)
+    block_last = jnp.stack(store, 0)
+    spare = all_to_all(block_last, mesh_ax, concat_axis=0, split_axis=0)
+    return jnp.concatenate(spare, 0)
 
 
 def with_halo(cells, sides, width):
@@ -85,9 +95,7 @@
     row_base = lax.axis_index("seq") * tok_count
     columns = layer_rows
     value_rows = jnp.dot(
-        columns,
-        lax.all_gather(value_weight, "dp", axis=0, tiled=True),
-        preferred_element_type=jnp.float32,
+        columns, _part_masks(value_weight, "dp"), preferred_element_type=jnp.float32
     )
     value_low = value_rows.astype(jnp.bfloat16)
     both_states = jnp.concatenate([key_states[0], value_low], axis=1)

time: 369 us -> 456 us (1.24)
  waiting for transfers between devices: 271 us -> 348 us
  starting transfers between devices: 13.2 us -> 21.4 us
    all_to_all x0 -> x1, waiting for transfers between devices: none -> 67 us  [_part_masks(): spare = all_to_all(block_last, mesh_ax, concat_axis=0, split_axis=0)]
    unnamed x4, waiting for transfers between devices: 117 us -> 127 us
    all_gather x1, waiting for transfers between devices: 66.7 us -> 57.4 us  [local(): lax.all_gather(value_weight, 'dp', axis=0, tiled=True)]
    reduce_scatter x1, waiting for transfers between devices: 59.7 us -> 67.6 us  [local(): summed = lax.psum_scatter(own_rows, 'seq', scatter_dimension=1, tiled=True)]
    all_to_all x0 -> x1, starting transfers between devices: none -> 7.41 us  [_part_masks(): spare = all_to_all(block_last, mesh_ax, concat_axis=0, split_axis=0)]
    unnamed x80 -> x90, local copies, waits for them, and re-layouts: 22.4 us -> 22 us
  transfers between devices with their start and end apart: 7 -> 8, of which waited for: 7 -> 8; matrix products, arithmetic and copies ran while one was open for 5% -> 4% of each run, Pallas kernels for 0% -> 0%
where the time goes in v1:
time: 456 us; the launch traced here: 455 us
  waiting for transfers between devices  348 us (76%)
  matrix products  38.2 us (8%)
  local copies, waits for them, and re-layouts  28.2 us (6%)
  starting transfers between devices  21.4 us (5%)
  between operations  14.3 us (3%)
  other arithmetic  4.92 us (1%)
    unnamed x4, waiting for transfers between devices  127 us
    reduce_scatter x1, waiting for transfers between devices, local(): summed = lax.psum_scatter(own_rows, 'seq', scatter_dimension=1, tiled=True)  67.6 us
    all_to_all x1, waiting for transfers between devices, _part_masks(): spare = all_to_all(block_last, mesh_ax, concat_axis=0, split_axis=0)  67 us
    all_gather x1, waiting for transfers between devices, local(): lax.all_gather(value_weight, 'dp', axis=0, tiled=True)  57.4 us
    unnamed x90, local copies, waits for them, and re-layouts  22 us
    ppermute x2, waiting for transfers between devices, passed_along(): return lax.ppermute(array, axis, pairs)  21.4 us
  transfers between devices with their start and end apart: 8, of which 8 were waited for; matrix products, arithmetic and copies ran while one was open for 4% of the time, Pallas kernels for 0%

profile of v1, /device:TPU:16, one launch (start us, length us, event | category | flops | bytes accessed | tf_op | source)
XLA Modules:
  0.0 455.3 jit_solution(14181386477449865617)
XLA Ops:
  7.2 3.9 stack.17
  11.1 7.4 %all-to-all-start = ((bf16[16,320,512]{2,1,0:T(8,128)(2,1)}), bf16[16,320,512]{2,1,0:T(8,128)(2,1)}, u32[]{:S(2)}, u32[]{:S(2)}) async-start(bf16[16,320,512]{2,1,0:T(8,128)(2,1)} %stack.17), calls=%async_computation | async-start | bytes 10485760 | tf_op jit(solution)/shard_map/all_to_all | solution.py:15
  18.8 67.0 %all-to-all-done = bf16[16,320,512]{2,1,0:T(8,128)(2,1)} async-done(((bf16[16,320,512]{2,1,0:T(8,128)(2,1)}), bf16[16,320,512]{2,1,0:T(8,128)(2,1)}, u32[]{:S(2)}, u32[]{:S(2)}) %all-to-all-start) | async-done | bytes 5242912 | tf_op jit(solution)/shard_map/all_to_all | solution.py:15
  85.8 3.4 fusion.36
  90.0 1.3 collective-permute-start.1
  91.3 6.1 %collective-permute-start = (bf16[128,1024]{1,0:T(8,128)(2,1)}, bf16[128,1024]{1,0:T(8,128)(2,1)}, u32[]{:S(2)}, u32[]{:S(2)}) collective-permute-start(bf16[128,1024]{1,0:T(8,128)(2,1)} %pad_maximum_fusion.2), channel_id=1, source_target_pairs={{0,1},{1,2},{2,3},{3,4},{4,5},{5,6},{6,7},{7,8},{8,9},{9,10},{10,1... | collective-permute-start | bytes 786440 | tf_op jit(solution)/shard_map/ppermute | solution.py:27
  100.2 2.0 collective-permute-done.1
  102.2 5.8 %collective-permute-done = bf16[128,1024]{1,0:T(8,128)(2,1)} collective-permute-done((bf16[128,1024]{1,0:T(8,128)(2,1)}, bf16[128,1024]{1,0:T(8,128)(2,1)}, u32[]{:S(2)}, u32[]{:S(2)}) %collective-permute-start) | collective-permute-done | bytes 262176 | tf_op jit(solution)/shard_map/ppermute | solution.py:27
  109.4 1.4 fusion.76
  111.4 1.4 fusion.80
  112.8 1.5 fusion.78
  114.3 1.4 fusion.79
  115.7 1.4 fusion.77
  117.1 1.3 multiply_reduce_fusion.3
  126.5 1.9 fusion.35
  128.4 1.8 fusion.34
  130.2 1.8 fusion.33
  132.0 1.8 fusion.32
  133.9 1.3 collective-permute-start.2
  135.2 5.2 %collective-permute-start.3 = (f32[128,1024]{0,1:T(8,128)S(1)}, f32[128,1024]{0,1:T(8,128)S(1)}, u32[]{:S(2)}, u32[]{:S(2)}) collective-permute-start(f32[128,1024]{0,1:T(8,128)S(1)} %get-tuple-element.21), channel_id=1, source_target_pairs={{0,1},{1,2},{2,3},{3,4},{4,5},{5,6},{6,7},{7,8},{8,9},{9,10},{10,1... | collective-permute-start | bytes 1572872 | tf_op jit(solution)/shard_map/ppermute | solution.py:39
  140.5 10.0 %collective-permute-done.2 = f32[128,1024]{0,1:T(8,128)S(1)} collective-permute-done((f32[128,1024]{0,1:T(8,128)S(1)}, f32[128,1024]{0,1:T(8,128)S(1)}, u32[]{:S(2)}, u32[]{:S(2)}) %collective-permute-start.2) | collective-permute-done | bytes 524320 | tf_op jit(solution)/shard_map/ppermute | solution.py:39
  150.5 11.4 %collective-permute-done.3 = f32[128,1024]{0,1:T(8,128)S(1)} collective-permute-done((f32[128,1024]{0,1:T(8,128)S(1)}, f32[128,1024]{0,1:T(8,128)S(1)}, u32[]{:S(2)}, u32[]{:S(2)}) %collective-permute-start.3) | collective-permute-done | bytes 524320 | tf_op jit(solution)/shard_map/ppermute | solution.py:39
  161.9 5.3 %convolution_bitcast_fusion = f32[5120,512]{0,1:T(8,128)} fusion(bf16[1,128,5120]{2,1,0:T(8,128)(2,1)S(1)} %copy-done, bf16[128,1024]{0,1:T(8,128)(2,1)S(1)} %fusion.52), kind=kOutput, calls=%fused_computation.4 | convolution fusion | flops 671088640 | bytes 11927552 | tf_op jit(solution)/shard_map/dot_general | solution.py:138
  167.3 11.4 %copy.205 = f32[5120,512]{1,0:T(8,128)} copy(f32[5120,512]{0,1:T(8,128)} %convolution_bitcast_fusion) | data formatting | bytes 20971520
  179.6 2.2 fusion.50
  181.8 126.3 %reduce-scatter.7.cloned.1.call-done = f32[320,512]{1,0:T(8,128)} async-done(((f32[5120,512]{1,0:T(8,128)}), f32[320,512]{1,0:T(8,128)}) %reduce-scatter.7.cloned.1.call-update) | async-done | bytes 655376
  308.0 2.3 copy.206
  310.4 2.3 fusion.48
  317.0 57.4 %all-gather.2.cloned.1.call-done = bf16[5120,512]{1,0:T(8,128)(2,1)} async-done(((bf16[320,512]{1,0:T(8,128)(2,1)}), bf16[5120,512]{1,0:T(8,128)(2,1)}) %all-gather.2.cloned.1.call-update) | async-done | bytes 5242896 | tf_op jit(solution)/shard_map/all_gather | solution.py:132
  374.4 5.4 %fusion.4 = bf16[1,128,5120]{2,1,0:T(8,128)(2,1)} fusion(bf16[5120,512]{1,0:T(8,128)(2,1)} %all-gather.2.cloned.1.call-done, bf16[128,1024]{0,1:T(8,128)(2,1)S(1)} %fusion.52), kind=kOutput, calls=%fused_computation.6 | convolution fusion | flops 671744000 | bytes 6684672 | tf_op jit(solution)/shard_map/dot_general | solution.py:130
  379.8 67.6 %reduce-scatter.5.cloned.1.call-done = f32[320,32]{0,1:T(8,128)} async-done(((f32[320,512]{0,1:T(8,128)}), f32[320,32]{0,1:T(8,128)}) %reduce-scatter.5.cloned.1.call-update) | async-done | bytes 40976 | tf_op jit(solution)/shard_map/reduce_scatter | solution.py:145
  447.4 1.4 broadcast_multiply_fusion
  (119 shorter events, 18.8 us)
Async XLA Ops:
  7.2 78.7 %copy-start = (bf16[1,128,5120]{2,1,0:T(8,128)(2,1)S(1)}, bf16[1,128,5120]{2,1,0:T(8,128)(2,1)}, u32[]{:S(2)}) copy-start(bf16[1,128,5120]{2,1,0:T(8,128)(2,1)} %param.7) | copy-start | bytes 3932164
  11.1 7.5 %copy-start.19 = (s32[1,2048]{1,0:T(1,128)S(1)}, s32[1,2048]{1,0:T(1,128)}, u32[]{:S(2)}) copy-start(s32[1,2048]{1,0:T(1,128)} %param.12) | copy-start | bytes 24580
  11.1 7.6 %copy-start.20 = (s32[1,32]{1,0:T(1,128)S(1)}, s32[1,32]{1,0:T(1,128)}, u32[]{:S(2)}) copy-start(s32[1,32]{1,0:T(1,128)} %param.13) | copy-start | bytes 388
  11.1 74.7 %all-to-all-start = ((bf16[16,320,512]{2,1,0:T(8,128)(2,1)}), bf16[16,320,512]{2,1,0:T(8,128)(2,1)}, u32[]{:S(2)}, u32[]{:S(2)}) async-start(bf16[16,320,512]{2,1,0:T(8,128)(2,1)} %stack.17), calls=%async_computation | async-start | bytes 10485760 | tf_op jit(solution)/shard_map/all_to_all | solution.py:15
  18.5 289.5 %reduce-scatter.7.cloned.1.call-start = ((), (), s32[]{:S(2)}) async-start(), calls=%async_computation.5 | async-start | bytes 11141120
  85.8 3.4 copy-start.6
  85.8 12.1 %copy-start.1 = (bf16[1,128,2560]{2,1,0:T(8,128)(2,1)S(1)}, bf16[1,128,2560]{2,1,0:T(8,128)(2,1)}, u32[]{:S(2)}) copy-start(bf16[1,128,2560]{2,1,0:T(8,128)(2,1)} %param.8) | copy-start | bytes 1966084
  89.2 9.0 %copy-start.2 = (bf16[1,128,2560]{2,1,0:T(8,128)(2,1)S(1)}, bf16[1,128,2560]{2,1,0:T(8,128)(2,1)}, u32[]{:S(2)}) copy-start(bf16[1,128,2560]{2,1,0:T(8,128)(2,1)} %param.10) | copy-start | bytes 1966084
  90.0 12.2 %collective-permute-start.1 = (bf16[128,1024]{1,0:T(8,128)(2,1)}, bf16[128,1024]{1,0:T(8,128)(2,1)}, u32[]{:S(2)}, u32[]{:S(2)}) collective-permute-start(bf16[128,1024]{1,0:T(8,128)(2,1)} %pad_maximum_fusion.2), channel_id=1, source_target_pairs={{1,0},{2,1},{3,2},{4,3},{5,4},{6,5},{7,6},{8,7},{9,8},{10,9},{11,1... | collective-permute-start | bytes 786440 | tf_op jit(solution)/shard_map/ppermute | solution.py:29
  91.3 16.7 %collective-permute-start = (bf16[128,1024]{1,0:T(8,128)(2,1)}, bf16[128,1024]{1,0:T(8,128)(2,1)}, u32[]{:S(2)}, u32[]{:S(2)}) collective-permute-start(bf16[128,1024]{1,0:T(8,128)(2,1)} %pad_maximum_fusion.2), channel_id=1, source_target_pairs={{0,1},{1,2},{2,3},{3,4},{4,5},{5,6},{6,7},{7,8},{8,9},{9,10},{10,1... | collective-permute-start | bytes 786440 | tf_op jit(solution)/shard_map/ppermute | solution.py:27
  98.2 17.5 %copy-start.3 = (bf16[1,128,2560]{1,2,0:T(8,128)(2,1)}, bf16[1,128,2560]{1,2,0:T(8,128)(2,1)S(1)}, u32[]{:S(2)}) copy-start(bf16[1,128,2560]{1,2,0:T(8,128)(2,1)S(1)} %copy.134) | copy-start | bytes 1966084
  100.2 15.5 %copy-start.18 = (pred[128,384]{0,1:T(8,128)(4,1)}, pred[128,384]{0,1:T(8,128)(4,1)S(1)}, u32[]{:S(2)}) copy-start(pred[128,384]{0,1:T(8,128)(4,1)S(1)} %or_and_fusion) | copy-start | bytes 147460
  111.3 2.9 copy-start.11
  111.4 2.9 copy-start.13
  111.4 2.9 copy-start.9
  111.4 20.7 %copy-start.7 = (bf16[384,1,128]{2,1,0:T(2,128)(2,1)}, bf16[384,1,128]{2,1,0:T(2,128)(2,1)S(1)}, u32[]{:S(2)}) copy-start(bf16[384,1,128]{2,1,0:T(2,128)(2,1)S(1)} %get-tuple-element.27) | copy-start | bytes 294916
  118.6 1.7 copy-start.25
  120.6 2.5 copy-start.30
  120.6 2.5 copy-start.36
  124.7 1.7 copy-start.38
  126.5 1.9 copy-start.10
  128.4 1.8 copy-start.12
  133.9 16.6 %collective-permute-start.2 = (f32[128,1024]{0,1:T(8,128)S(1)}, f32[128,1024]{0,1:T(8,128)S(1)}, u32[]{:S(2)}, u32[]{:S(2)}) collective-permute-start(f32[128,1024]{0,1:T(8,128)S(1)} %get-tuple-element.20), channel_id=1, source_target_pairs={{1,0},{2,1},{3,2},{4,3},{5,4},{6,5},{7,6},{8,7},{9,8},{10,9},{11,1... | collective-permute-start | bytes 1572872 | tf_op jit(solution)/shard_map/ppermute | solution.py:39
  135.2 26.6 %collective-permute-start.3 = (f32[128,1024]{0,1:T(8,128)S(1)}, f32[128,1024]{0,1:T(8,128)S(1)}, u32[]{:S(2)}, u32[]{:S(2)}) collective-permute-start(f32[128,1024]{0,1:T(8,128)S(1)} %get-tuple-element.21), channel_id=1, source_target_pairs={{0,1},{1,2},{2,3},{3,4},{4,5},{5,6},{6,7},{7,8},{8,9},{9,10},{10,1... | collective-permute-start | bytes 1572872 | tf_op jit(solution)/shard_map/ppermute | solution.py:39
  178.7 195.7 %all-gather.2.cloned.1.call-start = ((), (), s32[]{:S(2)}) async-start(), calls=%async_computation.3 | async-start | bytes 5570560 | tf_op jit(solution)/shard_map/all_gather | solution.py:132
  179.4 267.9 %reduce-scatter.5.cloned.1.call-start = ((), (), s32[]{:S(2)}) async-start(), calls=%async_computation.4 | async-start | bytes 835584 | tf_op jit(solution)/shard_map/reduce_scatter | solution.py:145
  181.8 128.6 %copy-start.37 = (f32[5,128]{1,0:T(8,128)S(1)}, f32[5,128]{1,0:T(8,128)}, u32[]{:S(2)}) copy-start(f32[5,128]{1,0:T(8,128)} %copy-done.36) | copy-start | bytes 7684
  310.3 2.3 copy-start.24
  310.3 2.3 copy-start.29
  310.4 2.3 copy-start.35
  312.7 1.6 copy-start.32
  312.7 1.6 copy-start.39
  (18 other events, 20.6 us)
Sparse Core Ops, SparseCore 0:
  178.8 129.1 reduce-scatter.6
  310.8 63.5 all-gather.1
  376.9 70.4 reduce-scatter.4
